TPU v7x, 32 devices: a whole 2x2x4 slice. The times are simulated.
32 devices in a mesh: rows: 8 (over z, x), grp: 4 (over y, core).
Axes of the slice: x: 2, y: 2, z: 4, core: 2. Of those that a mesh axis runs over, the one named last changes fastest.
Arguments:
- matrix: float32 [65536, 1024], P(('rows', 'grp'))
- row_signs: int32 [65536], P(('rows', 'grp')), may hold values from -1 to 1, as said below
- samples: int32 [8192], P(('rows', 'grp')), may hold values from 0 to 65535, as said below
Outputs:
- factor: float32 [1024, 1024], P('rows')
Inputs may be any that keep to these rules, and one draw needn't show every extreme that they name: `row_signs`: every entry is 1 or -1. `samples`: entries are distinct and increasing; entries k * 256 to (k + 1) * 256 - 1 lie in rows k * 2048 to (k + 1) * 2048 - 1.
All inputs are finite; a program needn't handle non-finite values.
Results may differ from a plain program's by a relative error of at most 0.00011.
Values sent between devices are 32-bit elements; how exact they have to be, the bound alone decides.
A program may use at most 128 MiB of HBM per device.

v0:
```python
import jax
import jax.numpy as jnp
from jax import lax
from jax.sharding import PartitionSpec as P

exact_mode = lax.Precision.HIGHEST


def parity_sign(left, right, length):
    correlation = left & right
    ones_total = jnp.zeros_like(correlation)
    for bit_level in range(max(1, length.bit_length() - 1)):
        ones_total = ones_total + (correlation >> bit_level & 1)
    return (1 - 2 * (ones_total % 2)).astype(jnp.float32)


def sylvester(length):
    indices = jnp.arange(length, dtype=jnp.int32)
    return parity_sign(indices[:, None], indices[None, :], length)


def shards(matrix, row_signs, samples):
    count_rows = lax.axis_size("rows")
    count_grp = lax.axis_size("grp")
    blocks = count_rows * count_grp
    row_dev, col_count = matrix.shape
    piece_rows = row_dev // blocks
    total_rows = row_dev * blocks
    sample_dev = samples.shape[0]
    position = lax.axis_index(("rows", "grp"))
    signed = matrix * row_signs.astype(jnp.float32)[:, None]
    before = jnp.dot(sylvester(row_dev), signed, precision=exact_mode)
    arrived = lax.all_to_all(
        lax.all_to_all(
            before.reshape(1, 1, row_dev, col_count),
            "rows",
            split_axis=2,
            concat_axis=0,
            tiled=True,
        ),
        "grp",
        split_axis=2,
        concat_axis=1,
        tiled=True,
    )
    mixed_rows = jnp.dot(
        sylvester(blocks), arrived.reshape(blocks, piece_rows * col_count), precision=exact_mode
    )
    mixed_rows = mixed_rows.reshape(count_rows, count_grp, piece_rows, col_count)
    mixed_rows = mixed_rows / jnp.sqrt(jnp.float32(total_rows))
    all_indices = lax.all_gather(samples, ("rows", "grp"), axis=0, tiled=True)
    owner_block = all_indices // row_dev
    within = all_indices % row_dev - position * piece_rows
    owner_hit = (owner_block[:, None] == jnp.arange(blocks, dtype=jnp.int32)[None, :]).astype(
        jnp.float32
    )
    local_hit = (within[:, None] == jnp.arange(piece_rows, dtype=jnp.int32)[None, :]).astype(
        jnp.float32
    )
    weights = jnp.einsum("kb,kt->bt", owner_hit, local_hit, precision=exact_mode).reshape(
        blocks * piece_rows
    )
    flat_rows = mixed_rows.reshape(blocks * piece_rows, col_count)
    local_gram = jnp.einsum(
        "kn,km->nm", flat_rows * weights[:, None], flat_rows, precision=exact_mode
    )
    summed_gram = lax.psum(local_gram, ("rows", "grp"))
    gram_total = summed_gram * (total_rows / (sample_dev * blocks))
    lower_factor = jnp.linalg.cholesky(gram_total)
    upper_factor = lower_factor.T
    share_rows = col_count // count_rows
    return lax.dynamic_slice_in_dim(
        upper_factor, lax.axis_index("rows") * share_rows, share_rows, 0
    )


def solution(mesh):
    return jax.shard_map(
        shards,
        mesh=mesh,
        in_specs=(P(("rows", "grp"), None), P(("rows", "grp")), P(("rows", "grp"))),
        out_specs=P("rows", None),
        check_vma=False,
    )
```

profile of v0, /device:TPU:0, one launch (start us, length us, event | category | flops | bytes accessed | tf_op | source)
XLA Modules:
  0.0 873.1 jit_solution(1184886997414699403)
XLA Ops:
  11.2 93.9 %fusion.26 = f32[1,1,2048,1024]{3,2,1,0:T(8,128)S(1)} fusion(f32[2048,1024]{1,0:T(8,128)S(1)} %fusion.115), kind=kOutput, calls=%fused_computation.29 | convolution fusion | flops 51736739840 | bytes 16777216 | tf_op jit(solution)/shard_map/dot_general | solution.py:32
  105.2 10.7 %copy.40 = f32[1,1,2048,1024]{3,1,0,2:T(1,128)S(1)} copy(f32[1,1,2048,1024]{3,2,1,0:T(8,128)S(1)} %fusion.26) | data formatting | bytes 16777216 | tf_op jit(solution)/shard_map/reshape | solution.py:35
  115.9 190.1 %all_to_all.21 = f32[1,1,2048,1024]{3,1,0,2:T(1,128)S(1)} all-to-all(f32[1,1,2048,1024]{3,1,0,2:T(1,128)S(1)} %copy.40), channel_id=1, replica_groups=mesh['rows'=8,'grp'=4] {'rows'}, dimensions={2} | all-to-all | bytes 16777216 | tf_op jit(solution)/shard_map/all_to_all | solution.py:34
  306.0 8.1 copy.41
  320.0 123.8 %all-gather = s32[32,1,256]{2,1,0:T(1,128)S(1)} all-gather(s32[1,1,256]{2,1,0:T(1,128)S(1)} %bitcast.77), channel_id=1, replica_groups=mesh['rows'=8,'grp'=4] {'rows','grp'}, dimensions={0}, use_global_device_ids=true | all-gather | bytes 33792 | tf_op jit(solution)/shard_map/all_gather | solution.py:51
  444.5 11.4 %copy.42 = f32[8,1,256,1024]{3,2,0,1:T(8,128)} copy(f32[8,1,256,1024]{3,0,1,2:T(8,128)} %all-to-all-done.1) | data formatting | bytes 16777216 | tf_op jit(solution)/shard_map/all_to_all | solution.py:33
  463.4 10.6 %fusion.9 = f32[8,4,64,1024]{3,0,2,1:T(8,128)S(1)} fusion(f32[4,64,8,1024]{3,2,1,0:T(8,128)} %bitcast.73, s32[8,4]{0,1:T(4,128)S(1)} %multiply_add_fusion), kind=kOutput, calls=%fused_computation.12 | convolution fusion | flops 805336064 | bytes 16777344 | tf_op jit(solution)/shard_map/dot_general | solution.py:46
  474.1 31.2 %fusion.35 = f32[1024,1024]{0,1:T(8,128)} fusion(f32[8,4,64,1024]{3,0,2,1:T(8,128)S(1)} %fusion.9, f32[8,4,64]{0,2,1:T(8,128)S(1)} %copy.44), kind=kOutput, calls=%fused_computation.35 | convolution fusion | flops 25773998080 | bytes 12591104 | tf_op jit(solution)/shard_map/kn,km->nm/dot_general | solution.py:64
  505.4 138.7 %all-reduce.3.cloned.1.call-done = f32[1024,1024]{0,1:T(8,128)} async-done(((f32[1024,1024]{0,1:T(8,128)}), f32[1024,1024]{0,1:T(8,128)}) %all-reduce.3.cloned.1.call-update) | async-done | bytes 4194320 | tf_op jit(solution)/shard_map/psum | solution.py:67
  660.8 11.7 %cholesky.223 = f32[128,128]{1,0:T(8,128)S(1)} custom-call(f32[128,128]{1,0:T(8,128)S(1)} %cholesky.580), custom_call_target="Cholesky" | custom-call | tf_op jit(solution)/shard_map/jit(cholesky)/cholesky | solution.py:69
  675.0 9.8 %custom-call.59 = f32[1,128,128]{1,2,0:T(8,128)S(1)} custom-call(f32[1,128,128]{2,1,0:T(8,128)S(1)} %get-tuple-element.26), custom_call_target="InvertDiagBlocksLowerTriangular" | custom-call | tf_op jit(solution)/shard_map/jit(cholesky)/cholesky | solution.py:69
  688.8 12.1 %cholesky.244 = f32[128,128]{1,0:T(8,128)S(1)} custom-call(f32[128,128]{1,0:T(8,128)S(1)} %cholesky.584), custom_call_target="Cholesky" | custom-call | tf_op jit(solution)/shard_map/jit(cholesky)/cholesky | solution.py:69
  701.5 9.8 %custom-call.60 = f32[1,128,128]{1,2,0:T(8,128)S(1)} custom-call(f32[1,128,128]{2,1,0:T(8,128)S(1)} %get-tuple-element.23), custom_call_target="InvertDiagBlocksLowerTriangular" | custom-call | tf_op jit(solution)/shard_map/jit(cholesky)/cholesky | solution.py:69
  714.7 11.7 %cholesky.468 = f32[128,128]{1,0:T(8,128)S(1)} custom-call(f32[128,128]{1,0:T(8,128)S(1)} %cholesky.589), custom_call_target="Cholesky" | custom-call | tf_op jit(solution)/shard_map/jit(cholesky)/cholesky | solution.py:69
  727.0 9.8 %custom-call.61 = f32[1,128,128]{1,2,0:T(8,128)S(1)} custom-call(f32[1,128,128]{2,1,0:T(8,128)S(1)} %get-tuple-element.20), custom_call_target="InvertDiagBlocksLowerTriangular" | custom-call | tf_op jit(solution)/shard_map/jit(cholesky)/cholesky | solution.py:69
  740.3 11.9 %cholesky.487 = f32[128,128]{1,0:T(8,128)S(1)} custom-call(f32[128,128]{1,0:T(8,128)S(1)} %cholesky.594), custom_call_target="Cholesky" | custom-call | tf_op jit(solution)/shard_map/jit(cholesky)/cholesky | solution.py:69
  752.9 9.8 %custom-call.62 = f32[1,128,128]{1,2,0:T(8,128)S(1)} custom-call(f32[1,128,128]{2,1,0:T(8,128)S(1)} %get-tuple-element.17), custom_call_target="InvertDiagBlocksLowerTriangular" | custom-call | tf_op jit(solution)/shard_map/jit(cholesky)/cholesky | solution.py:69
  766.1 11.7 %cholesky.506 = f32[128,128]{1,0:T(8,128)S(1)} custom-call(f32[128,128]{1,0:T(8,128)S(1)} %cholesky.599), custom_call_target="Cholesky" | custom-call | tf_op jit(solution)/shard_map/jit(cholesky)/cholesky | solution.py:69
  778.5 10.0 %custom-call.63 = f32[1,128,128]{1,2,0:T(8,128)S(1)} custom-call(f32[1,128,128]{2,1,0:T(8,128)S(1)} %get-tuple-element.14), custom_call_target="InvertDiagBlocksLowerTriangular" | custom-call | tf_op jit(solution)/shard_map/jit(cholesky)/cholesky | solution.py:69
  791.8 11.7 %cholesky.526 = f32[128,128]{1,0:T(8,128)S(1)} custom-call(f32[128,128]{1,0:T(8,128)S(1)} %cholesky.604), custom_call_target="Cholesky" | custom-call | tf_op jit(solution)/shard_map/jit(cholesky)/cholesky | solution.py:69
  804.2 9.8 %custom-call.64 = f32[1,128,128]{1,2,0:T(8,128)S(1)} custom-call(f32[1,128,128]{2,1,0:T(8,128)S(1)} %get-tuple-element.11), custom_call_target="InvertDiagBlocksLowerTriangular" | custom-call | tf_op jit(solution)/shard_map/jit(cholesky)/cholesky | solution.py:69
  817.0 11.7 %cholesky.546 = f32[128,128]{1,0:T(8,128)S(1)} custom-call(f32[128,128]{1,0:T(8,128)S(1)} %cholesky.609), custom_call_target="Cholesky" | custom-call | tf_op jit(solution)/shard_map/jit(cholesky)/cholesky | solution.py:69
  829.3 9.8 %custom-call.65 = f32[1,128,128]{1,2,0:T(8,128)S(1)} custom-call(f32[1,128,128]{2,1,0:T(8,128)S(1)} %get-tuple-element.8), custom_call_target="InvertDiagBlocksLowerTriangular" | custom-call | tf_op jit(solution)/shard_map/jit(cholesky)/cholesky | solution.py:69
  841.8 11.7 %cholesky.564 = f32[128,128]{1,0:T(8,128)S(1)} custom-call(f32[128,128]{1,0:T(8,128)S(1)} %convolution_subtract_fusion.6), custom_call_target="Cholesky" | custom-call | tf_op jit(solution)/shard_map/jit(cholesky)/cholesky | solution.py:69
  (57 shorter events, 72.3 us)
Async XLA Ops:
  314.1 5.9 copy-start.1
  314.1 130.4 %all-to-all-start.1 = ((f32[8,1,256,1024]{3,0,1,2:T(8,128)}), f32[8,1,256,1024]{3,0,1,2:T(8,128)}, u32[]{:S(2)}, u32[]{:S(2)}) async-start(f32[8,1,256,1024]{3,0,1,2:T(8,128)} %copy.41), calls=%async_computation.1 | async-start | bytes 16777216 | tf_op jit(solution)/shard_map/all_to_all | solution.py:33
  319.9 324.1 %all-reduce.3.cloned.1.call-start = ((), (), s32[]{:S(2)}) async-start(), calls=%async_computation.2 | async-start | bytes 8388608 | tf_op jit(solution)/shard_map/psum | solution.py:67
  658.8 1.9 copy-start
Sparse Core Ops, SparseCore 0:
  505.5 138.4 all-reduce.2
where the time goes:
time: 879 us; the launch traced here: 873 us
  blocking collectives  314 us (36%)
  other arithmetic  188 us (21%)
  matrix products  159 us (18%)
  waiting for transfers between devices  139 us (16%)
  local copies, waits for them, and re-layouts  48.6 us (6%)
  between operations  19.1 us (2%)
    all_to_all x1, blocking collectives, shards(): lax.all_to_all(before.reshape(1, 1, row_dev, col_count), 'rows', split_ax...  190 us
    another operation x30, other arithmetic, shards(): lower_factor = jnp.linalg.cholesky(gram_total)  172 us
    psum x1, waiting for transfers between devices, shards(): summed_gram = lax.psum(local_gram, ('rows', 'grp'))  139 us
    all_gather x1, blocking collectives, shards(): all_indices = lax.all_gather(samples, ('rows', 'grp'), axis=0, tiled=True)  124 us
    dot_general x1, matrix products, shards(): before = jnp.dot(sylvester(row_dev), signed, precision=exact_mode)  93.9 us
    dot_general x1, matrix products, shards(): jnp.einsum('kn,km->nm', flat_rows * weights[:, None], flat_rows, precisio...  31.2 us
    another operation x14, matrix products, shards(): lower_factor = jnp.linalg.cholesky(gram_total)  23.1 us
  transfers between devices with their start and end apart: 2, of which 1 were waited for; matrix products, arithmetic and copies ran while one was open for 0% of the time, Pallas kernels for 0%

commit v1 on v0

v1 whole, which is shorter than its diff:
```python
import functools

import jax
import jax.numpy as jnp
from jax import lax
from jax.experimental import pallas as pl
from jax.experimental.pallas import tpu as pltpu
from jax.sharding import PartitionSpec as P

exact_mode = lax.Precision.HIGHEST
VMEM_LIMIT = 60 * 1024 * 1024
TILE = 128


def sylvester(length):
    matrix = jnp.ones((1, 1), jnp.float32)
    while matrix.shape[0] < length:
        matrix = jnp.block([[matrix, matrix], [matrix, -matrix]])
    return matrix


def butterfly(parts):
    span = 1
    while span < len(parts):
        parts = list(parts)
        for start in range(0, len(parts), 2 * span):
            for i in range(start, start + span):
                low, high = parts[i], parts[i + span]
                parts[i], parts[i + span] = low + high, low - high
        span *= 2
    return parts


def split(x):
    high = x.astype(jnp.bfloat16)
    return high, (x - high.astype(jnp.float32)).astype(jnp.bfloat16)


def local_kernel(base, x_ref, s_ref, h_ref, o_ref):
    parts = []
    for i in range(x_ref.shape[0] // base):
        rows = slice(i * base, (i + 1) * base)
        high, low = split(x_ref[rows, :] * s_ref[rows, :])
        both = jnp.dot(h_ref[...], high, preferred_element_type=jnp.float32)
        both += jnp.dot(h_ref[...], low, preferred_element_type=jnp.float32)
        parts.append(both)
    for i, part in enumerate(butterfly(parts)):
        o_ref[i * base : (i + 1) * base, :] = part


def local_transform(matrix, signs, base):
    rows, cols = matrix.shape
    return pl.pallas_call(
        functools.partial(local_kernel, base),
        grid=(cols // TILE,),
        out_shape=jax.ShapeDtypeStruct((rows, cols), jnp.float32),
        in_specs=[
            pl.BlockSpec((rows, TILE), lambda c: (0, c)),
            pl.BlockSpec((rows, TILE), lambda c: (0, 0)),
            pl.BlockSpec((base, base), lambda c: (0, 0)),
        ],
        out_specs=pl.BlockSpec((rows, TILE), lambda c: (0, c)),
        compiler_params=pltpu.CompilerParams(vmem_limit_bytes=VMEM_LIMIT),
    )(matrix, signs, sylvester(base).astype(jnp.bfloat16))


def gram_kernel(scale, x_ref, w_ref, o_ref, left, right):
    blocks, step, cols = x_ref.shape
    rows = blocks * step

    @pl.when(pl.program_id(0) == 0)
    def _():
        o_ref[...] = jnp.zeros_like(o_ref)

    def mix(c, carry):
        at = pl.ds(pl.multiple_of(c * TILE, TILE), TILE)
        parts = butterfly([x_ref[b, :, at] for b in range(blocks)])
        for b in range(0, blocks, 2):
            x = jnp.concatenate(parts[b : b + 2], axis=0) * scale
            w = jnp.concatenate([w_ref[b], w_ref[b + 1]], axis=0)
            high, low = split(x)
            here = slice(b * step, (b + 2) * step)
            there = slice(rows + b * step, rows + (b + 2) * step)
            masked = (high.astype(jnp.float32) * w).astype(jnp.bfloat16)
            left[here, at] = masked
            right[here, at] = high
            left[there, at] = masked
            right[there, at] = (2.0 * low.astype(jnp.float32)).astype(jnp.bfloat16)
        return carry

    lax.fori_loop(0, cols // TILE, mix, 0)
    wide = 2 * TILE

    def add(n, carry):
        at = pl.ds(pl.multiple_of(n * wide, wide), wide)
        o_ref[:, at] += lax.dot_general(
            left[...], right[:, at], (((0,), (0,)), ((), ())), preferred_element_type=jnp.float32
        )
        return carry

    lax.fori_loop(0, cols // wide, add, 0)


def gram_share(arrived, weights, scale):
    blocks, piece, cols = arrived.shape
    step = 8
    return pl.pallas_call(
        functools.partial(gram_kernel, scale),
        grid=(piece // step,),
        out_shape=jax.ShapeDtypeStruct((cols, cols), jnp.float32),
        in_specs=[
            pl.BlockSpec((blocks, step, cols), lambda t: (0, t, 0)),
            pl.BlockSpec((blocks, step, TILE), lambda t: (0, t, 0)),
        ],
        out_specs=pl.BlockSpec((cols, cols), lambda t: (0, 0)),
        scratch_shapes=[pltpu.VMEM((2 * blocks * step, cols), jnp.bfloat16)] * 2,
        compiler_params=pltpu.CompilerParams(vmem_limit_bytes=VMEM_LIMIT),
    )(arrived, weights)


def factor_kernel(g_ref, u_ref, work):
    cols = g_ref.shape[0]
    work[...] = g_ref[...]
    row_id = lax.broadcasted_iota(jnp.int32, (TILE, TILE), 0)
    lane_id = lax.broadcasted_iota(jnp.int32, (TILE, TILE), 1)

    def panel(k, carry):
        base = pl.multiple_of(k * TILE, TILE)
        here = pl.ds(base, TILE)
        block = work[here, here]
        strips = [block[i : i + 8, :] for i in range(0, TILE, 8)]
        unit = (row_id == lane_id).astype(jnp.float32)
        inverse = [unit[i : i + 8, :] for i in range(0, TILE, 8)]
        sub_id = lax.broadcasted_iota(jnp.int32, (8, TILE), 0)
        for j in range(TILE):
            s, r = divmod(j, 8)
            row = strips[s][r : r + 1, :]
            inv_row = inverse[s][r : r + 1, :]
            root = lax.rsqrt(jnp.broadcast_to(row[:, j : j + 1], (1, TILE)))
            row = row * root
            inv_row = inv_row * root
            for i in range(s, TILE // 8):
                column = jnp.broadcast_to(strips[i][:, j : j + 1], (8, TILE)) * root
                if i == s:
                    column = jnp.where(sub_id > r, column, 0.0)
                strips[i] = strips[i] - column * row
                inverse[i] = inverse[i] - column * inv_row
                if i == s:
                    inverse[i] = jnp.where(sub_id == r, inv_row, inverse[i])
        lower_inverse = jnp.concatenate(inverse, axis=0)
        lower_inverse = jnp.where(lane_id <= row_id, lower_inverse, 0.0)
        wide_row = lax.broadcasted_iota(jnp.int32, (TILE, cols), 0) + base
        wide_lane = lax.broadcasted_iota(jnp.int32, (TILE, cols), 1)
        upper = jnp.dot(
            lower_inverse, work[here, :], precision=exact_mode, preferred_element_type=jnp.float32
        )
        u_ref[here, :] = jnp.where(wide_lane >= wide_row, upper, 0.0)

        def trail(i, inner):
            there = pl.ds(pl.multiple_of(i * TILE, TILE), TILE)
            work[there, :] -= lax.dot_general(
                u_ref[here, there],
                u_ref[here, :],
                (((0,), (0,)), ((), ())),
                precision=exact_mode,
                preferred_element_type=jnp.float32,
            )
            return inner

        lax.fori_loop(k + 1, cols // TILE, trail, 0)
        return carry

    lax.fori_loop(0, cols // TILE, panel, 0)


def factorize(gram):
    return pl.pallas_call(
        factor_kernel,
        out_shape=jax.ShapeDtypeStruct(gram.shape, jnp.float32),
        in_specs=[pl.BlockSpec(memory_space=pltpu.VMEM)],
        out_specs=pl.BlockSpec(memory_space=pltpu.VMEM),
        scratch_shapes=[pltpu.VMEM(gram.shape, jnp.float32)],
        compiler_params=pltpu.CompilerParams(vmem_limit_bytes=VMEM_LIMIT),
    )(gram)


def shards(matrix, row_signs, samples):
    count_rows = lax.axis_size("rows")
    blocks = count_rows * lax.axis_size("grp")
    row_dev, col_count = matrix.shape
    piece_rows = row_dev // blocks
    sample_dev = samples.shape[0]
    position = lax.axis_index(("rows", "grp"))
    all_indices = lax.all_gather(samples, ("rows", "grp"), axis=0)
    signs = jnp.broadcast_to(row_signs.astype(jnp.float32)[:, None], (row_dev, TILE))
    before = local_transform(matrix, signs, min(256, row_dev))
    arrived = lax.all_to_all(
        before.reshape(blocks, piece_rows, col_count),
        ("rows", "grp"),
        split_axis=0,
        concat_axis=0,
        tiled=True,
    )
    first = jnp.arange(blocks, dtype=jnp.int32)[:, None] * row_dev + position * piece_rows
    within = all_indices - first
    hits = within[:, None, :] == jnp.arange(piece_rows, dtype=jnp.int32)[None, :, None]
    weights = jnp.max(hits.astype(jnp.float32), axis=2)
    weights = jnp.broadcast_to(weights[:, :, None], (blocks, piece_rows, TILE))
    scale = (sample_dev * blocks) ** -0.5
    half = gram_share(arrived, weights, scale)
    summed = lax.psum((half + half.T) * 0.5, ("rows", "grp"))
    upper_factor = factorize(summed)
    share_rows = col_count // count_rows
    return lax.dynamic_slice_in_dim(
        upper_factor, lax.axis_index("rows") * share_rows, share_rows, 0
    )


def solution(mesh):
    return jax.shard_map(
        shards,
        mesh=mesh,
        in_specs=(P(("rows", "grp"), None), P(("rows", "grp")), P(("rows", "grp"))),
        out_specs=P("rows", None),
        check_vma=False,
    )
```

time: 879 us -> 544 us (0.62)
  other arithmetic: 188 us -> 7.99 us
  matrix products: 159 us -> 0 us
  Pallas kernels: 0 us -> 151 us
  blocking collectives: 314 us -> 177 us
  local copies, waits for them, and re-layouts: 48.6 us -> 9.93 us
  waiting for transfers between devices: 139 us -> 177 us
    all_to_all x1 -> x0, blocking collectives: 190 us -> none  [shards(): lax.all_to_all(before.reshape(1, 1, row_dev, col_count), 'rows', split_ax...]
    another operation x30 -> x0, other arithmetic: 172 us -> none  [shards(): lower_factor = jnp.linalg.cholesky(gram_total)]
    pallas_call x0 -> x3, Pallas kernels: none -> 151 us  [the longest x1 112 us: factorize(): pl.pallas_call(factor_kernel, out_shape=jax.ShapeDtypeStruct(gram.shape,...]
    dot_general x4 -> x0, matrix products: 136 us -> none  [the longest x1 93.9 us: shards(): before = jnp.dot(sylvester(row_dev), signed, precision=exact_mode)]
    all_gather x1, blocking collectives: 124 us -> 177 us  [shards(): all_indices = lax.all_gather(samples, ('rows', 'grp'), axis=0)]
    psum x1, waiting for transfers between devices: 139 us -> 170 us  [shards(): summed = lax.psum((half + half.T) * 0.5, ('rows', 'grp'))]
    another operation x14 -> x0, matrix products: 23.1 us -> none  [shards(): lower_factor = jnp.linalg.cholesky(gram_total)]
    all_to_all x2 -> x0, local copies, waits for them, and re-layouts: 19.5 us -> none  [the longest x1 11.4 us: shards(): lax.all_to_all(lax.all_to_all(before.reshape(1, 1, row_dev, col_count), '...]
  transfers between devices with their start and end apart: 2 -> 2, of which waited for: 1 -> 2; matrix products, arithmetic and copies ran while one was open for 0% -> 0% of each run, Pallas kernels for 0% -> 0%
where the time goes in v1:
time: 544 us
  blocking collectives  177 us (33%)
  waiting for transfers between devices  177 us (33%)
  Pallas kernels  151 us (28%)
  between operations  13.4 us (2%)
  local copies, waits for them, and re-layouts  9.93 us (2%)
  other arithmetic  7.99 us (1%)
  starting transfers between devices  7.5 us (1%)
    all_gather x1, blocking collectives, shards(): all_indices = lax.all_gather(samples, ('rows', 'grp'), axis=0)  177 us
    psum x1, waiting for transfers between devices, shards(): summed = lax.psum((half + half.T) * 0.5, ('rows', 'grp'))  170 us
    pallas_call x1, Pallas kernels, factorize(): pl.pallas_call(factor_kernel, out_shape=jax.ShapeDtypeStruct(gram.shape,...  112 us
    pallas_call x1, Pallas kernels, gram_share(): pl.pallas_call(functools.partial(gram_kernel, scale), grid=(piece // step...  27.6 us
    pallas_call x1, Pallas kernels, local_transform(): pl.pallas_call(functools.partial(local_kernel, base), grid=(cols // TILE,...  11.3 us
  transfers between devices with their start and end apart: 2, of which 2 were waited for; matrix products, arithmetic and copies ran while one was open for 0% of the time, Pallas kernels for 0%

profile of v1, /device:TPU:0, one launch (start us, length us, event | category | flops | bytes accessed | tf_op | source)
XLA Modules:
  0.0 543.7 jit_solution(12235611422791284264)
XLA Ops:
  6.5 0.7 convert_element_type.7
  7.2 1.3 broadcast_in_dim.4.s_ref
  8.6 11.3 %shard_map.37 = f32[2048,1024]{1,0:T(8,128)} custom-call(f32[2048,1024]{1,0:T(8,128)} %x_ref.1, f32[2048,128]{1,0:T(8,128)} %broadcast_in_dim.4.s_ref, bf16[256,256]{1,0:T(8,128)(2,1)} %constant.48.clone.1.h_ref), custom_call_target="tpu_custom_call" | custom-call | tf_op jit(solution)/shard_map/pallas_call | solution.py:53
  19.9 0.0 copy-start
  19.9 7.5 %all-to-all-start = ((f32[32,64,1024]{2,1,0:T(8,128)}), f32[32,64,1024]{2,1,0:T(8,128)}, u32[]{:S(2)}, u32[]{:S(2)}) async-start(f32[32,64,1024]{2,1,0:T(8,128)} %bitcast.8), calls=%async_computation | async-start | bytes 16777216 | tf_op jit(solution)/shard_map/all_to_all | solution.py:197
  27.3 0.0 all-reduce.2.cloned.1.call-start
  27.4 0.0 copy-done
  27.4 177.0 %all-gather.1 = s32[32,1,256]{2,1,0:T(1,128)S(1)} all-gather(s32[1,1,256]{2,1,0:T(1,128)S(1)} %bitcast.9), channel_id=2, replica_groups=mesh['rows'=8,'grp'=4] {'rows','grp'}, dimensions={0}, use_global_device_ids=true | all-gather | bytes 33792 | tf_op jit(solution)/shard_map/all_gather | solution.py:194
  204.4 0.1 bitcast_subtract_fusion
  204.5 0.3 convert_reduce_fusion
  204.8 7.7 %all-to-all-done.x_ref = f32[32,64,1024]{2,1,0:T(8,128)} async-done(((f32[32,64,1024]{2,1,0:T(8,128)}), f32[32,64,1024]{2,1,0:T(8,128)}, u32[]{:S(2)}, u32[]{:S(2)}) %all-to-all-start) | async-done | bytes 8388640 | tf_op jit(solution)/shard_map/all_to_all | solution.py:197
  212.5 1.4 broadcast_in_dim.5.w_ref
  213.9 27.6 %shard_map.38 = f32[1024,1024]{1,0:T(8,128)} custom-call(f32[32,64,1024]{2,1,0:T(8,128)} %all-to-all-done.x_ref, f32[32,64,128]{2,1,0:T(8,128)} %broadcast_in_dim.5.w_ref), custom_call_target="tpu_custom_call" | custom-call | tf_op jit(solution)/shard_map/pallas_call | solution.py:107
  241.4 5.4 copy.6
  246.8 6.9 %fusion = f32[1024,1024]{1,0:T(8,128)} fusion(f32[1024,1024]{1,0:T(8,128)} %shard_map.38, f32[1024,1024]{0,1:T(8,128)} %copy.6), kind=kLoop, calls=%fused_computation.1 | loop fusion | flops 2097152 | bytes 12582912 | tf_op jit(solution)/shard_map/mul | solution.py:211
  253.7 0.0 all-reduce.2.cloned.1.call-update
  253.7 169.6 %all-reduce.2.cloned.1.call-done.g_ref = f32[1024,1024]{1,0:T(8,128)} async-done(((f32[1024,1024]{1,0:T(8,128)}), f32[1024,1024]{1,0:T(8,128)}) %all-reduce.2.cloned.1.call-update) | async-done | bytes 4194320 | tf_op jit(solution)/shard_map/psum | solution.py:211
  423.3 111.7 %shard_map.39 = f32[1024,1024]{1,0:T(8,128)} custom-call(f32[1024,1024]{1,0:T(8,128)} %all-reduce.2.cloned.1.call-done.g_ref), custom_call_target="tpu_custom_call" | custom-call | tf_op jit(solution)/shard_map/pallas_call | solution.py:177
  535.0 1.9 constant_dynamic-slice_fusion
  (1 shorter events, 0.0 us)
Async XLA Ops:
  19.9 7.5 %copy-start = (s32[256]{0:T(256)S(1)}, s32[256]{0:T(256)}, u32[]{:S(2)}) copy-start(s32[256]{0:T(256)} %param.5) | copy-start | bytes 3076
  19.9 192.6 %all-to-all-start = ((f32[32,64,1024]{2,1,0:T(8,128)}), f32[32,64,1024]{2,1,0:T(8,128)}, u32[]{:S(2)}, u32[]{:S(2)}) async-start(f32[32,64,1024]{2,1,0:T(8,128)} %bitcast.8), calls=%async_computation | async-start | bytes 16777216 | tf_op jit(solution)/shard_map/all_to_all | solution.py:197
  27.3 396.0 %all-reduce.2.cloned.1.call-start = ((), (), s32[]{:S(2)}) async-start(), calls=%async_computation.1 | async-start | bytes 8388608 | tf_op jit(solution)/shard_map/psum | solution.py:211
Sparse Core Ops, SparseCore 0:
  253.8 169.4 all-reduce.1

commit v2 on v1

--- a/solution.py
+++ b/solution.py
@@ -118,9 +118,15 @@
     )(arrived, weights)
 
 
+def upper_tiles(cols):
+    return [(i, j) for i in range(0, cols, TILE) for j in range(i, cols, TILE)]
+
+
 def factor_kernel(g_ref, u_ref, work):
-    cols = g_ref.shape[0]
-    work[...] = g_ref[...]
+    cols = u_ref.shape[0]
+    work[...] = jnp.zeros_like(work)
+    for p, (i, j) in enumerate(upper_tiles(cols)):
+        work[i : i + TILE, j : j + TILE] = g_ref[p * TILE : (p + 1) * TILE, :]
     row_id = lax.broadcasted_iota(jnp.int32, (TILE, TILE), 0)
     lane_id = lax.broadcasted_iota(jnp.int32, (TILE, TILE), 1)
 
@@ -173,15 +179,15 @@
     lax.fori_loop(0, cols // TILE, panel, 0)
 
 
-def factorize(gram):
+def factorize(packed, cols):
     return pl.pallas_call(
         factor_kernel,
-        out_shape=jax.ShapeDtypeStruct(gram.shape, jnp.float32),
+        out_shape=jax.ShapeDtypeStruct((cols, cols), jnp.float32),
         in_specs=[pl.BlockSpec(memory_space=pltpu.VMEM)],
         out_specs=pl.BlockSpec(memory_space=pltpu.VMEM),
-        scratch_shapes=[pltpu.VMEM(gram.shape, jnp.float32)],
+        scratch_shapes=[pltpu.VMEM((cols, cols), jnp.float32)],
         compiler_params=pltpu.CompilerParams(vmem_limit_bytes=VMEM_LIMIT),
-    )(gram)
+    )(packed)
 
 
 def shards(matrix, row_signs, samples):
@@ -208,8 +214,12 @@
     weights = jnp.broadcast_to(weights[:, :, None], (blocks, piece_rows, TILE))
     scale = (sample_dev * blocks) ** -0.5
     half = gram_share(arrived, weights, scale)
-    summed = lax.psum((half + half.T) * 0.5, ("rows", "grp"))
-    upper_factor = factorize(summed)
+    whole = (half + half.T) * 0.5
+    packed = jnp.concatenate(
+        [whole[i : i + TILE, j : j + TILE] for i, j in upper_tiles(col_count)], axis=0
+    )
+    summed = lax.psum(packed, ("rows", "grp"))
+    upper_factor = factorize(summed, col_count)
     share_rows = col_count // count_rows
     return lax.dynamic_slice_in_dim(
         upper_factor, lax.axis_index("rows") * share_rows, share_rows, 0

time: 544 us -> 537 us (0.987)
  waiting for transfers between devices: 177 us -> 170 us
    psum x1, waiting for transfers between devices: 170 us -> 163 us  [shards(): summed = lax.psum(packed, ('rows', 'grp'))]
where the time goes in v2:
time: 537 us; the launch traced here: 536 us
  blocking collectives  177 us (33%)
  waiting for transfers between devices  170 us (32%)
  Pallas kernels  150 us (28%)
  between operations  13.7 us (3%)
  local copies, waits for them, and re-layouts  11.7 us (2%)
  starting transfers between devices  7.49 us (1%)
  other arithmetic  5.56 us (1%)
    all_gather x1, blocking collectives, shards(): all_indices = lax.all_gather(samples, ('rows', 'grp'), axis=0)  177 us
    psum x1, waiting for transfers between devices, shards(): summed = lax.psum(packed, ('rows', 'grp'))  163 us
    pallas_call x1, Pallas kernels, factorize(): pl.pallas_call(factor_kernel, out_shape=jax.ShapeDtypeStruct((cols, cols)...  111 us
    pallas_call x1, Pallas kernels, gram_share(): pl.pallas_call(functools.partial(gram_kernel, scale), grid=(piece // step...  27.5 us
    pallas_call x1, Pallas kernels, local_transform(): pl.pallas_call(functools.partial(local_kernel, base), grid=(cols // TILE,...  11.3 us
  transfers between devices with their start and end apart: 2, of which 2 were waited for; matrix products, arithmetic and copies ran while one was open for 0% of the time, Pallas kernels for 0%

profile of v2, /device:TPU:0, one launch (start us, length us, event | category | flops | bytes accessed | tf_op | source)
XLA Modules:
  0.0 536.0 jit_solution(18233841418340778915)
XLA Ops:
  6.5 0.7 convert_element_type.7
  7.2 1.3 broadcast_in_dim.4.s_ref
  8.5 11.3 %shard_map.37 = f32[2048,1024]{1,0:T(8,128)} custom-call(f32[2048,1024]{1,0:T(8,128)} %x_ref.1, f32[2048,128]{1,0:T(8,128)} %broadcast_in_dim.4.s_ref, bf16[256,256]{1,0:T(8,128)(2,1)} %constant.48.clone.1.h_ref), custom_call_target="tpu_custom_call" | custom-call | tf_op jit(solution)/shard_map/pallas_call | solution.py:53
  19.9 0.0 copy-start.1
  19.9 7.4 %all-to-all-start = ((f32[32,64,1024]{2,1,0:T(8,128)}), f32[32,64,1024]{2,1,0:T(8,128)}, u32[]{:S(2)}, u32[]{:S(2)}) async-start(f32[32,64,1024]{2,1,0:T(8,128)} %bitcast.8), calls=%async_computation | async-start | bytes 16777216 | tf_op jit(solution)/shard_map/all_to_all | solution.py:203
  27.3 0.0 all-reduce.2.cloned.1.call-start
  27.4 0.0 copy-done.1
  27.4 177.0 %all-gather.1 = s32[32,1,256]{2,1,0:T(1,128)S(1)} all-gather(s32[1,1,256]{2,1,0:T(1,128)S(1)} %bitcast.9), channel_id=2, replica_groups=mesh['rows'=8,'grp'=4] {'rows','grp'}, dimensions={0}, use_global_device_ids=true | all-gather | bytes 33792 | tf_op jit(solution)/shard_map/all_gather | solution.py:200
  204.4 0.1 bitcast_subtract_fusion
  204.4 0.3 convert_reduce_fusion
  204.8 7.7 %all-to-all-done.x_ref = f32[32,64,1024]{2,1,0:T(8,128)} async-done(((f32[32,64,1024]{2,1,0:T(8,128)}), f32[32,64,1024]{2,1,0:T(8,128)}, u32[]{:S(2)}, u32[]{:S(2)}) %all-to-all-start) | async-done | bytes 8388640 | tf_op jit(solution)/shard_map/all_to_all | solution.py:203
  212.5 1.4 broadcast_in_dim.5.w_ref
  213.9 27.5 %shard_map.38 = f32[1024,1024]{1,0:T(8,128)} custom-call(f32[32,64,1024]{2,1,0:T(8,128)} %all-to-all-done.x_ref, f32[32,64,128]{2,1,0:T(8,128)} %broadcast_in_dim.5.w_ref), custom_call_target="tpu_custom_call" | custom-call | tf_op jit(solution)/shard_map/pallas_call | solution.py:107
  241.4 5.3 copy.6
  246.8 4.4 fusion
  251.9 0.0 copy-start
  251.9 1.4 copy-done
  253.3 0.0 all-reduce.2.cloned.1.call-update
  253.3 162.7 %all-reduce.2.cloned.1.call-done.g_ref = f32[4608,128]{1,0:T(8,128)} async-done(((f32[4608,128]{1,0:T(8,128)}), f32[4608,128]{1,0:T(8,128)}) %all-reduce.2.cloned.1.call-update) | async-done | bytes 2359312 | tf_op jit(solution)/shard_map/psum | solution.py:221
  416.0 111.3 %shard_map.39 = f32[1024,1024]{1,0:T(8,128)} custom-call(f32[4608,128]{1,0:T(8,128)} %all-reduce.2.cloned.1.call-done.g_ref), custom_call_target="tpu_custom_call" | custom-call | tf_op jit(solution)/shard_map/pallas_call | solution.py:183
  527.3 1.9 constant_dynamic-slice_fusion
  (36 shorter events, 0.4 us)
Async XLA Ops:
  19.9 7.5 %copy-start.1 = (s32[256]{0:T(256)S(1)}, s32[256]{0:T(256)}, u32[]{:S(2)}) copy-start(s32[256]{0:T(256)} %param.5) | copy-start | bytes 3076
  19.9 192.6 %all-to-all-start = ((f32[32,64,1024]{2,1,0:T(8,128)}), f32[32,64,1024]{2,1,0:T(8,128)}, u32[]{:S(2)}, u32[]{:S(2)}) async-start(f32[32,64,1024]{2,1,0:T(8,128)} %bitcast.8), calls=%async_computation | async-start | bytes 16777216 | tf_op jit(solution)/shard_map/all_to_all | solution.py:203
  27.3 388.7 %all-reduce.2.cloned.1.call-start = ((), (), s32[]{:S(2)}) async-start(), calls=%async_computation.1 | async-start | bytes 4718592 | tf_op jit(solution)/shard_map/psum | solution.py:221
  251.9 1.4 copy-start
Sparse Core Ops, SparseCore 0:
  253.4 162.5 all-reduce.1
